TPU v7x, 512 devices: a whole 4x8x8 slice. The times are simulated.
512 devices in a mesh: sample: 4 (over y_lo), variant: 32 (over x, z), trait: 4 (over y_hi, core).
Axes of the slice: x: 4, y: 8 (y_hi: 2, y_lo: 4; y = y_hi * 4 + y_lo), z: 8, core: 2. Of those that a mesh axis runs over, the one named last changes fastest.
Arguments:
- dosages: bfloat16 [4096, 65536], P('sample', 'variant')
- phenotypes: float32 [4096, 64], P('sample', 'trait')
- batch_rows: int32 [8, 4096], P(None, 'sample'), may hold values from 0 to 1023
Outputs:
- weights: float32 [64, 65536], P('trait', 'variant')
Inputs may be any that keep to these rules, and one draw needn't show every extreme that they name: Draw j of iteration t refers to sample (j // 1024) * 1024 + batch_rows[t-1, j]; draws repeat.
All inputs are finite; a program needn't handle non-finite values.
Results may differ from a plain program's by a relative error of at most 0.0025.
Values may be sent and summed in bfloat16 or wider, within the bound.
A program may use at most 64 MiB of HBM per device.

v0:
```python
import math
import jax
import jax.numpy as jnp
from jax import lax
from jax.sharding import PartitionSpec as P

ITERS = 8


def trait_power(dual):
    squares = jnp.sum(dual * dual, axis=0)
    return lax.psum(squares, "trait")


def on_device(dosages, phenotypes, batch_rows):
    local_rows = dosages.shape[0]
    group_size = lax.axis_size("sample")
    total_variants = dosages.shape[1] * lax.axis_size("variant")
    total_draws = batch_rows.shape[1] * group_size
    pred_scale = 0.06 * math.sqrt(total_draws) / total_variants
    grad_scale = 1.0 / math.sqrt(total_draws)
    width_traits = phenotypes.shape[1]
    width_cols = dosages.shape[1]
    dual = jnp.zeros((width_traits, width_cols), jnp.float32)
    weights_full = jnp.zeros((width_traits, width_cols), jnp.float32)
    weights_low = weights_full.astype(jnp.bfloat16)
    for step in range(ITERS):
        turn = step + 1
        counts = jnp.zeros((local_rows,), jnp.float32).at[batch_rows[step]].add(1.0)
        if step == 0:
            predictions = jnp.zeros_like(phenotypes)
        else:
            partial_sum = lax.dot_general(
                dosages, weights_low, (((1,), (1,)), ((), ())), preferred_element_type=jnp.float32
            )
            predictions = (
                lax.psum(partial_sum.astype(jnp.bfloat16), "variant").astype(jnp.float32)
                * pred_scale
            )
        misfit = (counts[:, None] * (predictions - phenotypes)).astype(jnp.bfloat16)
        grad_part = lax.dot_general(
            misfit, dosages, (((0,), (0,)), ((), ())), preferred_element_type=jnp.float32
        )
        gradient = lax.psum(grad_part, "sample") * grad_scale
        dual = dual + (gradient - dual) / turn
        power = trait_power(dual)
        shrink = jax.nn.relu(1.0 - 20.0 / jnp.sqrt(power + 1e-05))
        weights_full = -math.sqrt(turn) * shrink[None, :] * dual
        weights_low = weights_full.astype(jnp.bfloat16)
    return weights_full


def solution(mesh):
    return jax.shard_map(
        on_device,
        mesh=mesh,
        in_specs=(P("sample", "variant"), P("sample", "trait"), P(None, "sample")),
        out_specs=P("trait", "variant"),
        check_vma=False,
    )
```

profile of v0, /device:TPU:1, one launch (start us, length us, event | category | flops | bytes accessed | tf_op | source)
XLA Modules:
  0.0 1546.0 jit_solution(12416131265628424412)
XLA Ops:
  6.5 1.1 compare_select_fusion
  7.6 7.6 scatter_custom_fusion
  15.3 3.6 fusion.14
  18.9 7.6 scatter_custom_fusion.1
  26.6 49.9 %all-reduce.9.cloned.1.call-done = f32[16,2048]{1,0:T(8,128)} async-done(((f32[16,2048]{1,0:T(8,128)}), f32[16,2048]{1,0:T(8,128)}) %all-reduce.9.cloned.1.call-update) | async-done | bytes 131088 | tf_op jit(solution)/shard_map/psum | solution.py:44
  77.4 11.7 psum.162
  89.2 3.5 fusion
  92.7 116.2 %psum.163 = bf16[1024,16]{0,1:T(8,128)(2,1)S(1)} all-reduce(bf16[1024,16]{0,1:T(8,128)(2,1)S(1)} %fusion), channel_id=1, replica_groups=mesh['sample'=4,'variant'=32,'trait'=4] {'variant'}, use_global_device_ids=true, to_apply=%region_5.6 | all-reduce | flops 16384 | bytes 65536 | tf_op jit(solution)/shard_map/psum | solution.py:37
  208.9 3.5 fusion.15
  212.4 7.6 scatter_custom_fusion.2
  220.1 63.4 %all-reduce.11.cloned.1.call-done = f32[16,2048]{1,0:T(8,128)} async-done(((f32[16,2048]{1,0:T(8,128)}), f32[16,2048]{1,0:T(8,128)}) %all-reduce.11.cloned.1.call-update) | async-done | bytes 131088 | tf_op jit(solution)/shard_map/psum | solution.py:44
  284.4 11.7 psum.165
  296.2 3.4 fusion.1
  299.5 116.2 %psum.166 = bf16[1024,16]{0,1:T(8,128)(2,1)S(1)} all-reduce(bf16[1024,16]{0,1:T(8,128)(2,1)S(1)} %fusion.1), channel_id=1, replica_groups=mesh['sample'=4,'variant'=32,'trait'=4] {'variant'}, use_global_device_ids=true, to_apply=%region_10.11 | all-reduce | flops 16384 | bytes 65536 | tf_op jit(solution)/shard_map/psum | solution.py:37
  415.7 3.5 fusion.16
  419.3 7.6 scatter_custom_fusion.3
  426.9 63.4 %all-reduce.13.cloned.1.call-done = f32[16,2048]{1,0:T(8,128)} async-done(((f32[16,2048]{1,0:T(8,128)}), f32[16,2048]{1,0:T(8,128)}) %all-reduce.13.cloned.1.call-update) | async-done | bytes 131088 | tf_op jit(solution)/shard_map/psum | solution.py:44
  491.3 11.7 psum.168
  503.0 3.5 fusion.2
  506.5 116.2 %psum.169 = bf16[1024,16]{0,1:T(8,128)(2,1)S(1)} all-reduce(bf16[1024,16]{0,1:T(8,128)(2,1)S(1)} %fusion.2), channel_id=1, replica_groups=mesh['sample'=4,'variant'=32,'trait'=4] {'variant'}, use_global_device_ids=true, to_apply=%region_15.16 | all-reduce | flops 16384 | bytes 65536 | tf_op jit(solution)/shard_map/psum | solution.py:37
  622.7 3.5 fusion.17
  626.4 7.6 scatter_custom_fusion.4
  634.1 63.2 %all-reduce.15.cloned.1.call-done = f32[16,2048]{1,0:T(8,128)} async-done(((f32[16,2048]{1,0:T(8,128)}), f32[16,2048]{1,0:T(8,128)}) %all-reduce.15.cloned.1.call-update) | async-done | bytes 131088 | tf_op jit(solution)/shard_map/psum | solution.py:44
  698.3 11.7 psum.171
  710.0 3.4 fusion.3
  713.4 116.2 %psum.172 = bf16[1024,16]{0,1:T(8,128)(2,1)S(1)} all-reduce(bf16[1024,16]{0,1:T(8,128)(2,1)S(1)} %fusion.3), channel_id=1, replica_groups=mesh['sample'=4,'variant'=32,'trait'=4] {'variant'}, use_global_device_ids=true, to_apply=%region_20.21 | all-reduce | flops 16384 | bytes 65536 | tf_op jit(solution)/shard_map/psum | solution.py:37
  829.6 3.5 fusion.18
  833.1 7.6 scatter_custom_fusion.5
  840.8 63.4 %all-reduce.17.cloned.1.call-done = f32[16,2048]{1,0:T(8,128)} async-done(((f32[16,2048]{1,0:T(8,128)}), f32[16,2048]{1,0:T(8,128)}) %all-reduce.17.cloned.1.call-update) | async-done | bytes 131088 | tf_op jit(solution)/shard_map/psum | solution.py:44
  905.1 11.7 psum.174
  916.9 3.5 fusion.4
  920.4 116.2 %psum.175 = bf16[1024,16]{0,1:T(8,128)(2,1)S(1)} all-reduce(bf16[1024,16]{0,1:T(8,128)(2,1)S(1)} %fusion.4), channel_id=1, replica_groups=mesh['sample'=4,'variant'=32,'trait'=4] {'variant'}, use_global_device_ids=true, to_apply=%region_25.26 | all-reduce | flops 16384 | bytes 65536 | tf_op jit(solution)/shard_map/psum | solution.py:37
  1036.5 3.5 fusion.19
  1040.1 7.6 scatter_custom_fusion.6
  1047.7 63.4 %all-reduce.19.cloned.1.call-done = f32[16,2048]{1,0:T(8,128)} async-done(((f32[16,2048]{1,0:T(8,128)}), f32[16,2048]{1,0:T(8,128)}) %all-reduce.19.cloned.1.call-update) | async-done | bytes 131088 | tf_op jit(solution)/shard_map/psum | solution.py:44
  1112.1 11.7 psum.177
  1123.9 3.4 fusion.5
  1127.2 116.2 %psum.178 = bf16[1024,16]{0,1:T(8,128)(2,1)S(1)} all-reduce(bf16[1024,16]{0,1:T(8,128)(2,1)S(1)} %fusion.5), channel_id=1, replica_groups=mesh['sample'=4,'variant'=32,'trait'=4] {'variant'}, use_global_device_ids=true, to_apply=%region_30.31 | all-reduce | flops 16384 | bytes 65536 | tf_op jit(solution)/shard_map/psum | solution.py:37
  1243.4 3.5 fusion.20
  1247.0 7.6 scatter_custom_fusion.7
  1254.6 63.4 %all-reduce.21.cloned.1.call-done = f32[16,2048]{1,0:T(8,128)} async-done(((f32[16,2048]{1,0:T(8,128)}), f32[16,2048]{1,0:T(8,128)}) %all-reduce.21.cloned.1.call-update) | async-done | bytes 131088 | tf_op jit(solution)/shard_map/psum | solution.py:44
  1319.0 11.7 psum.180
  1330.7 3.4 fusion.6
  1334.1 116.2 %psum.181 = bf16[1024,16]{0,1:T(8,128)(2,1)S(1)} all-reduce(bf16[1024,16]{0,1:T(8,128)(2,1)S(1)} %fusion.6), channel_id=1, replica_groups=mesh['sample'=4,'variant'=32,'trait'=4] {'variant'}, use_global_device_ids=true, to_apply=%region_35.36 | all-reduce | flops 16384 | bytes 65536 | tf_op jit(solution)/shard_map/psum | solution.py:37
  1450.3 3.5 fusion.21
  1453.8 71.1 %all-reduce.23.cloned.1.call-done = f32[16,2048]{1,0:T(8,128)} async-done(((f32[16,2048]{1,0:T(8,128)}), f32[16,2048]{1,0:T(8,128)}) %all-reduce.23.cloned.1.call-update) | async-done | bytes 131088 | tf_op jit(solution)/shard_map/psum | solution.py:44
  1525.8 11.7 psum.183
  1537.6 1.6 broadcast_multiply_fusion
  (41 shorter events, 8.3 us)
Async XLA Ops:
  6.5 70.0 %all-reduce.9.cloned.1.call-start = ((), (), s32[]{:S(2)}) async-start(), calls=%async_computation | async-start | bytes 262144 | tf_op jit(solution)/shard_map/psum | solution.py:44
  15.3 193.6 %copy-start = (f32[1024,16]{0,1:T(8,128)S(1)}, f32[1024,16]{0,1:T(8,128)}, u32[]{:S(2)}) copy-start(f32[1024,16]{0,1:T(8,128)} %param.4) | copy-start | bytes 196612
  18.9 264.6 %all-reduce.11.cloned.1.call-start = ((), (), s32[]{:S(2)}) async-start(), calls=%async_computation.1 | async-start | bytes 262144 | tf_op jit(solution)/shard_map/psum | solution.py:44
  89.2 194.3 %copy-start.1 = (f32[16,2048]{1,0:T(8,128)S(1)}, f32[16,2048]{1,0:T(8,128)}, u32[]{:S(2)}) copy-start(f32[16,2048]{1,0:T(8,128)} %all-reduce.9.cloned.1.call-done) | copy-start | bytes 393220
  212.4 277.9 %all-reduce.13.cloned.1.call-start = ((), (), s32[]{:S(2)}) async-start(), calls=%async_computation.2 | async-start | bytes 262144 | tf_op jit(solution)/shard_map/psum | solution.py:44
  419.2 278.0 %all-reduce.15.cloned.1.call-start = ((), (), s32[]{:S(2)}) async-start(), calls=%async_computation.3 | async-start | bytes 262144 | tf_op jit(solution)/shard_map/psum | solution.py:44
  503.0 194.3 %copy-start.2 = (f32[16,2048]{1,0:T(8,128)S(1)}, f32[16,2048]{1,0:T(8,128)}, u32[]{:S(2)}) copy-start(f32[16,2048]{1,0:T(8,128)} %all-reduce.13.cloned.1.call-done) | copy-start | bytes 393220
  626.2 277.9 %all-reduce.17.cloned.1.call-start = ((), (), s32[]{:S(2)}) async-start(), calls=%async_computation.4 | async-start | bytes 262144 | tf_op jit(solution)/shard_map/psum | solution.py:44
  833.1 278.0 %all-reduce.19.cloned.1.call-start = ((), (), s32[]{:S(2)}) async-start(), calls=%async_computation.5 | async-start | bytes 262144 | tf_op jit(solution)/shard_map/psum | solution.py:44
  916.9 194.3 %copy-start.3 = (f32[16,2048]{1,0:T(8,128)S(1)}, f32[16,2048]{1,0:T(8,128)}, u32[]{:S(2)}) copy-start(f32[16,2048]{1,0:T(8,128)} %all-reduce.17.cloned.1.call-done) | copy-start | bytes 393220
  1040.1 277.9 %all-reduce.21.cloned.1.call-start = ((), (), s32[]{:S(2)}) async-start(), calls=%async_computation.6 | async-start | bytes 262144 | tf_op jit(solution)/shard_map/psum | solution.py:44
  1246.9 277.9 %all-reduce.23.cloned.1.call-start = ((), (), s32[]{:S(2)}) async-start(), calls=%async_computation.7 | async-start | bytes 262144 | tf_op jit(solution)/shard_map/psum | solution.py:44
Sparse Core Ops, SparseCore 0:
  19.0 57.4 all-reduce.8
  212.5 70.9 all-reduce.10
  419.4 70.9 all-reduce.12
  626.3 70.9 all-reduce.14
  833.2 70.9 all-reduce.16
  1040.2 70.9 all-reduce.18
  1247.1 70.9 all-reduce.20
  1453.9 70.9 all-reduce.22
where the time goes:
time: 1550 us
  blocking collectives  907 us (59%)
  waiting for transfers between devices  501 us (32%)
  other arithmetic  71.3 us (5%)
  matrix products  52 us (3%)
    psum x7, blocking collectives, on_device(): lax.psum(partial_sum.astype(jnp.bfloat16), 'variant').astype(jnp.float32)  813 us
    psum x8, waiting for transfers between devices, on_device(): gradient = lax.psum(grad_part, 'sample') * grad_scale  501 us
    psum x8, blocking collectives, trait_power(): return lax.psum(squares, 'trait')  93.8 us
    scatter-add x8, other arithmetic, on_device(): counts = jnp.zeros((local_rows,), jnp.float32).at[batch_rows[step]].add(1.0)  60.9 us
  transfers between devices with their start and end apart: 8, of which 8 were waited for; matrix products, arithmetic and copies ran while one was open for 3% of the time, Pallas kernels for 0%

commit v1 on v0

--- a/solution.py
+++ b/solution.py
@@ -3,6 +3,7 @@
 import jax.numpy as jnp
 from jax import lax
 from jax.sharding import PartitionSpec as P
+from jax.lax import all_gather
 
 ITERS = 8
 
@@ -33,8 +34,9 @@
             partial_sum = lax.dot_general(
                 dosages, weights_low, (((1,), (1,)), ((), ())), preferred_element_type=jnp.float32
             )
+            _edit_array = lambda my_data, mesh_ax: jnp.sum(all_gather(my_data, mesh_ax), axis=0)
             predictions = (
-                lax.psum(partial_sum.astype(jnp.bfloat16), "variant").astype(jnp.float32)
+                _edit_array(partial_sum.astype(jnp.bfloat16), "variant").astype(jnp.float32)
                 * pred_scale
             )
         misfit = (counts[:, None] * (predictions - phenotypes)).astype(jnp.bfloat16)

time: 1550 us -> 1170 us (0.75)
  blocking collectives: 907 us -> 93.8 us
  waiting for transfers between devices: 501 us -> 921 us
    psum x7 -> x0, blocking collectives: 813 us -> none  [on_device(): lax.psum(partial_sum.astype(jnp.bfloat16), 'variant').astype(jnp.float32)]
    all_gather x0 -> x7, waiting for transfers between devices: none -> 482 us  [on_device(): all_gather(my_data, mesh_ax)]
    psum x8, waiting for transfers between devices: 501 us -> 439 us  [on_device(): gradient = lax.psum(grad_part, 'sample') * grad_scale]
  transfers between devices with their start and end apart: 8 -> 15, of which waited for: 8 -> 15; matrix products, arithmetic and copies ran while one was open for 3% -> 5% of each run, Pallas kernels for 0% -> 0%
where the time goes in v1:
time: 1170 us
  waiting for transfers between devices  921 us (79%)
  blocking collectives  93.8 us (8%)
  other arithmetic  73.9 us (6%)
  matrix products  56.4 us (5%)
  between operations  13.6 us (1%)
  local copies, waits for them, and re-layouts  12.6 us (1%)
    all_gather x7, waiting for transfers between devices, on_device(): all_gather(my_data, mesh_ax)  482 us
    psum x8, waiting for transfers between devices, on_device(): gradient = lax.psum(grad_part, 'sample') * grad_scale  439 us
    psum x8, blocking collectives, trait_power(): return lax.psum(squares, 'trait')  93.8 us
    scatter-add x8, other arithmetic, on_device(): counts = jnp.zeros((local_rows,), jnp.float32).at[batch_rows[step]].add(1.0)  60.9 us
    dot_general x7, matrix products, on_device(): lax.dot_general(dosages, weights_low, (((1,), (1,)), ((), ())), preferred...  28.3 us
    dot_general x8, matrix products, on_device(): lax.dot_general(misfit, dosages, (((0,), (0,)), ((), ())), preferred_elem...  28.1 us
  transfers between devices with their start and end apart: 15, of which 15 were waited for; matrix products, arithmetic and copies ran while one was open for 5% of the time, Pallas kernels for 0%

profile of v1, /device:TPU:1, one launch (start us, length us, event | category | flops | bytes accessed | tf_op | source)
XLA Modules:
  0.0 1172.5 jit_solution(12466238087528474747)
XLA Ops:
  7.7 7.6 scatter_custom_fusion
  15.3 3.5 fusion.14
  19.0 57.6 %all-reduce.9.cloned.1.call-done = f32[16,2048]{1,0:T(8,128)} async-done(((f32[16,2048]{1,0:T(8,128)}), f32[16,2048]{1,0:T(8,128)}) %all-reduce.9.cloned.1.call-update) | async-done | bytes 131088 | tf_op jit(solution)/shard_map/psum | solution.py:46
  77.5 11.7 %psum.113 = f32[2048]{0:T(1024)S(1)} all-reduce(f32[2048]{0:T(1024)S(1)} %multiply_reduce_fusion.7), channel_id=1, replica_groups=mesh['sample'=4,'variant'=32,'trait'=4] {'trait'}, use_global_device_ids=true, to_apply=%region_4.5 | all-reduce | flops 2048 | bytes 16384 | tf_op jit(solution)/shard_map/psum | solution.py:13
  89.2 4.1 fusion
  93.4 7.6 scatter_custom_fusion.1
  101.0 68.9 %all-gather.15.cloned.1.call-done = bf16[32768,16]{0,1:T(8,128)(2,1)} async-done(((bf16[1024,16]{0,1:T(8,128)(2,1)}), bf16[32768,16]{0,1:T(8,128)(2,1)}) %all-gather.15.cloned.1.call-update) | async-done | bytes 1048592 | tf_op jit(solution)/shard_map/all_gather | solution.py:37
  169.9 1.8 copy.4
  172.1 3.5 fusion.15
  175.7 54.5 %all-reduce.11.cloned.1.call-done = f32[16,2048]{1,0:T(8,128)} async-done(((f32[16,2048]{1,0:T(8,128)}), f32[16,2048]{1,0:T(8,128)}) %all-reduce.11.cloned.1.call-update) | async-done | bytes 131088 | tf_op jit(solution)/shard_map/psum | solution.py:46
  231.1 11.7 %psum.115 = f32[2048]{0:T(1024)S(1)} all-reduce(f32[2048]{0:T(1024)S(1)} %get-tuple-element.11), channel_id=1, replica_groups=mesh['sample'=4,'variant'=32,'trait'=4] {'trait'}, use_global_device_ids=true, to_apply=%region_9.10 | all-reduce | flops 2048 | bytes 16384 | tf_op jit(solution)/shard_map/psum | solution.py:13
  242.9 4.0 fusion.1
  246.9 7.6 scatter_custom_fusion.2
  254.6 68.9 %all-gather.17.cloned.1.call-done = bf16[32768,16]{0,1:T(8,128)(2,1)} async-done(((bf16[1024,16]{0,1:T(8,128)(2,1)}), bf16[32768,16]{0,1:T(8,128)(2,1)}) %all-gather.17.cloned.1.call-update) | async-done | bytes 1048592 | tf_op jit(solution)/shard_map/all_gather | solution.py:37
  323.5 1.8 copy.5
  325.6 3.5 fusion.16
  329.2 54.5 %all-reduce.13.cloned.1.call-done = f32[16,2048]{1,0:T(8,128)} async-done(((f32[16,2048]{1,0:T(8,128)}), f32[16,2048]{1,0:T(8,128)}) %all-reduce.13.cloned.1.call-update) | async-done | bytes 131088 | tf_op jit(solution)/shard_map/psum | solution.py:46
  384.7 11.7 %psum.117 = f32[2048]{0:T(1024)S(1)} all-reduce(f32[2048]{0:T(1024)S(1)} %multiply_reduce_fusion.5), channel_id=1, replica_groups=mesh['sample'=4,'variant'=32,'trait'=4] {'trait'}, use_global_device_ids=true, to_apply=%region_14.15 | all-reduce | flops 2048 | bytes 16384 | tf_op jit(solution)/shard_map/psum | solution.py:13
  396.4 4.1 fusion.2
  400.8 7.6 scatter_custom_fusion.3
  408.4 68.7 %all-gather.19.cloned.1.call-done = bf16[32768,16]{0,1:T(8,128)(2,1)} async-done(((bf16[1024,16]{0,1:T(8,128)(2,1)}), bf16[32768,16]{0,1:T(8,128)(2,1)}) %all-gather.19.cloned.1.call-update) | async-done | bytes 1048592 | tf_op jit(solution)/shard_map/all_gather | solution.py:37
  479.3 3.5 fusion.17
  482.9 54.5 %all-reduce.15.cloned.1.call-done = f32[16,2048]{1,0:T(8,128)} async-done(((f32[16,2048]{1,0:T(8,128)}), f32[16,2048]{1,0:T(8,128)}) %all-reduce.15.cloned.1.call-update) | async-done | bytes 131088 | tf_op jit(solution)/shard_map/psum | solution.py:46
  538.3 11.7 %psum.119 = f32[2048]{0:T(1024)S(1)} all-reduce(f32[2048]{0:T(1024)S(1)} %get-tuple-element.9), channel_id=1, replica_groups=mesh['sample'=4,'variant'=32,'trait'=4] {'trait'}, use_global_device_ids=true, to_apply=%region_19.20 | all-reduce | flops 2048 | bytes 16384 | tf_op jit(solution)/shard_map/psum | solution.py:13
  550.1 4.0 fusion.3
  554.1 7.6 scatter_custom_fusion.4
  561.8 68.9 %all-gather.21.cloned.1.call-done = bf16[32768,16]{0,1:T(8,128)(2,1)} async-done(((bf16[1024,16]{0,1:T(8,128)(2,1)}), bf16[32768,16]{0,1:T(8,128)(2,1)}) %all-gather.21.cloned.1.call-update) | async-done | bytes 1048592 | tf_op jit(solution)/shard_map/all_gather | solution.py:37
  632.8 3.5 fusion.18
  636.4 54.5 %all-reduce.17.cloned.1.call-done = f32[16,2048]{1,0:T(8,128)} async-done(((f32[16,2048]{1,0:T(8,128)}), f32[16,2048]{1,0:T(8,128)}) %all-reduce.17.cloned.1.call-update) | async-done | bytes 131088 | tf_op jit(solution)/shard_map/psum | solution.py:46
  691.9 11.7 %psum.121 = f32[2048]{0:T(1024)S(1)} all-reduce(f32[2048]{0:T(1024)S(1)} %multiply_reduce_fusion.3), channel_id=1, replica_groups=mesh['sample'=4,'variant'=32,'trait'=4] {'trait'}, use_global_device_ids=true, to_apply=%region_24.25 | all-reduce | flops 2048 | bytes 16384 | tf_op jit(solution)/shard_map/psum | solution.py:13
  703.6 4.1 fusion.4
  707.8 7.6 scatter_custom_fusion.5
  715.4 68.9 %all-gather.23.cloned.1.call-done = bf16[32768,16]{0,1:T(8,128)(2,1)} async-done(((bf16[1024,16]{0,1:T(8,128)(2,1)}), bf16[32768,16]{0,1:T(8,128)(2,1)}) %all-gather.23.cloned.1.call-update) | async-done | bytes 1048592 | tf_op jit(solution)/shard_map/all_gather | solution.py:37
  786.5 3.5 fusion.19
  790.1 54.5 %all-reduce.19.cloned.1.call-done = f32[16,2048]{1,0:T(8,128)} async-done(((f32[16,2048]{1,0:T(8,128)}), f32[16,2048]{1,0:T(8,128)}) %all-reduce.19.cloned.1.call-update) | async-done | bytes 131088 | tf_op jit(solution)/shard_map/psum | solution.py:46
  845.5 11.7 %psum.123 = f32[2048]{0:T(1024)S(1)} all-reduce(f32[2048]{0:T(1024)S(1)} %get-tuple-element.7), channel_id=1, replica_groups=mesh['sample'=4,'variant'=32,'trait'=4] {'trait'}, use_global_device_ids=true, to_apply=%region_29.30 | all-reduce | flops 2048 | bytes 16384 | tf_op jit(solution)/shard_map/psum | solution.py:13
  857.3 4.0 fusion.5
  861.6 7.6 scatter_custom_fusion.6
  869.2 68.7 %all-gather.25.cloned.1.call-done = bf16[32768,16]{0,1:T(8,128)(2,1)} async-done(((bf16[1024,16]{0,1:T(8,128)(2,1)}), bf16[32768,16]{0,1:T(8,128)(2,1)}) %all-gather.25.cloned.1.call-update) | async-done | bytes 1048592 | tf_op jit(solution)/shard_map/all_gather | solution.py:37
  940.0 3.5 fusion.20
  943.6 54.5 %all-reduce.21.cloned.1.call-done = f32[16,2048]{1,0:T(8,128)} async-done(((f32[16,2048]{1,0:T(8,128)}), f32[16,2048]{1,0:T(8,128)}) %all-reduce.21.cloned.1.call-update) | async-done | bytes 131088 | tf_op jit(solution)/shard_map/psum | solution.py:46
  999.1 11.7 %psum.125 = f32[2048]{0:T(1024)S(1)} all-reduce(f32[2048]{0:T(1024)S(1)} %get-tuple-element.5), channel_id=1, replica_groups=mesh['sample'=4,'variant'=32,'trait'=4] {'trait'}, use_global_device_ids=true, to_apply=%region_34.35 | all-reduce | flops 2048 | bytes 16384 | tf_op jit(solution)/shard_map/psum | solution.py:13
  1010.8 4.0 fusion.6
  1014.9 7.6 scatter_custom_fusion.7
  1022.5 68.9 %all-gather.27.cloned.1.call-done = bf16[32768,16]{0,1:T(8,128)(2,1)} async-done(((bf16[1024,16]{0,1:T(8,128)(2,1)}), bf16[32768,16]{0,1:T(8,128)(2,1)}) %all-gather.27.cloned.1.call-update) | async-done | bytes 1048592 | tf_op jit(solution)/shard_map/all_gather | solution.py:37
  1093.6 3.5 fusion.21
  1097.1 54.5 %all-reduce.23.cloned.1.call-done = f32[16,2048]{1,0:T(8,128)} async-done(((f32[16,2048]{1,0:T(8,128)}), f32[16,2048]{1,0:T(8,128)}) %all-reduce.23.cloned.1.call-update) | async-done | bytes 131088 | tf_op jit(solution)/shard_map/psum | solution.py:46
  1152.6 11.7 %psum.127 = f32[2048]{0:T(1024)S(1)} all-reduce(f32[2048]{0:T(1024)S(1)} %multiply_reduce_fusion), channel_id=1, replica_groups=mesh['sample'=4,'variant'=32,'trait'=4] {'trait'}, use_global_device_ids=true, to_apply=%region_38.39 | all-reduce | flops 2048 | bytes 16384 | tf_op jit(solution)/shard_map/psum | solution.py:13
  (69 shorter events, 23.2 us)
Async XLA Ops:
  6.5 70.0 %all-reduce.9.cloned.1.call-start = ((), (), s32[]{:S(2)}) async-start(), calls=%async_computation | async-start | bytes 262144 | tf_op jit(solution)/shard_map/psum | solution.py:46
  18.9 153.2 %copy-start = (f32[1024,16]{0,1:T(8,128)S(1)}, f32[1024,16]{0,1:T(8,128)}, u32[]{:S(2)}) copy-start(f32[1024,16]{0,1:T(8,128)} %param.4) | copy-start | bytes 196612
  18.9 151.0 %all-gather.15.cloned.1.call-start = ((), (), s32[]{:S(2)}) async-start(), calls=%async_computation.8 | async-start | bytes 1081344 | tf_op jit(solution)/shard_map/all_gather | solution.py:37
  93.3 136.9 %copy-start.1 = (f32[16,2048]{1,0:T(8,128)S(1)}, f32[16,2048]{1,0:T(8,128)}, u32[]{:S(2)}) copy-start(f32[16,2048]{1,0:T(8,128)} %all-reduce.9.cloned.1.call-done) | copy-start | bytes 393220
  93.3 136.8 %all-reduce.11.cloned.1.call-start = ((), (), s32[]{:S(2)}) async-start(), calls=%async_computation.1 | async-start | bytes 262144 | tf_op jit(solution)/shard_map/psum | solution.py:46
  175.6 147.9 %all-gather.17.cloned.1.call-start = ((), (), s32[]{:S(2)}) async-start(), calls=%async_computation.9 | async-start | bytes 1081344 | tf_op jit(solution)/shard_map/all_gather | solution.py:37
  246.9 136.8 %all-reduce.13.cloned.1.call-start = ((), (), s32[]{:S(2)}) async-start(), calls=%async_computation.2 | async-start | bytes 262144 | tf_op jit(solution)/shard_map/psum | solution.py:46
  329.2 147.9 %all-gather.19.cloned.1.call-start = ((), (), s32[]{:S(2)}) async-start(), calls=%async_computation.10 | async-start | bytes 1081344 | tf_op jit(solution)/shard_map/all_gather | solution.py:37
  400.5 136.8 %copy-start.2 = (f32[16,2048]{1,0:T(8,128)S(1)}, f32[16,2048]{1,0:T(8,128)}, u32[]{:S(2)}) copy-start(f32[16,2048]{1,0:T(8,128)} %all-reduce.13.cloned.1.call-done) | copy-start | bytes 393220
  400.5 136.8 %all-reduce.15.cloned.1.call-start = ((), (), s32[]{:S(2)}) async-start(), calls=%async_computation.3 | async-start | bytes 262144 | tf_op jit(solution)/shard_map/psum | solution.py:46
  482.8 147.9 %all-gather.21.cloned.1.call-start = ((), (), s32[]{:S(2)}) async-start(), calls=%async_computation.11 | async-start | bytes 1081344 | tf_op jit(solution)/shard_map/all_gather | solution.py:37
  554.1 136.8 %all-reduce.17.cloned.1.call-start = ((), (), s32[]{:S(2)}) async-start(), calls=%async_computation.4 | async-start | bytes 262144 | tf_op jit(solution)/shard_map/psum | solution.py:46
  636.4 147.9 %all-gather.23.cloned.1.call-start = ((), (), s32[]{:S(2)}) async-start(), calls=%async_computation.12 | async-start | bytes 1081344 | tf_op jit(solution)/shard_map/all_gather | solution.py:37
  707.7 136.8 %copy-start.3 = (f32[16,2048]{1,0:T(8,128)S(1)}, f32[16,2048]{1,0:T(8,128)}, u32[]{:S(2)}) copy-start(f32[16,2048]{1,0:T(8,128)} %all-reduce.17.cloned.1.call-done) | copy-start | bytes 393220
  707.7 136.8 %all-reduce.19.cloned.1.call-start = ((), (), s32[]{:S(2)}) async-start(), calls=%async_computation.5 | async-start | bytes 262144 | tf_op jit(solution)/shard_map/psum | solution.py:46
  790.0 147.9 %all-gather.25.cloned.1.call-start = ((), (), s32[]{:S(2)}) async-start(), calls=%async_computation.13 | async-start | bytes 1081344 | tf_op jit(solution)/shard_map/all_gather | solution.py:37
  861.3 136.8 %all-reduce.21.cloned.1.call-start = ((), (), s32[]{:S(2)}) async-start(), calls=%async_computation.6 | async-start | bytes 262144 | tf_op jit(solution)/shard_map/psum | solution.py:46
  943.6 147.9 %all-gather.27.cloned.1.call-start = ((), (), s32[]{:S(2)}) async-start(), calls=%async_computation.14 | async-start | bytes 1081344 | tf_op jit(solution)/shard_map/all_gather | solution.py:37
  1014.8 136.8 %all-reduce.23.cloned.1.call-start = ((), (), s32[]{:S(2)}) async-start(), calls=%async_computation.7 | async-start | bytes 262144 | tf_op jit(solution)/shard_map/psum | solution.py:46
Sparse Core Ops, SparseCore 0:
  19.0 57.4 all-reduce.8
  93.5 76.4 all-gather.14
  175.7 54.3 all-reduce.10
  247.0 76.4 all-gather.16
  329.3 54.3 all-reduce.12
  400.6 76.4 all-gather.18
  482.9 54.3 all-reduce.14
  554.2 76.4 all-gather.20
  636.5 54.3 all-reduce.16
  707.8 76.4 all-gather.22
  790.1 54.3 all-reduce.18
  861.4 76.4 all-gather.24
  943.7 54.3 all-reduce.20
  1015.0 76.4 all-gather.26
  1097.2 54.3 all-reduce.22
